TPU v7x, 512 devices: a whole 4x8x8 slice. The times are simulated.
512 devices in a mesh: context: 8 (over z), expert: 32 (over x, y), dp: 2 (over core).
Axes of the slice: x: 4, y: 8, z: 8, core: 2. Of those that a mesh axis runs over, the one named last changes fastest.
Arguments:
- residual: bfloat16 [32768, 1024], P(('dp', 'expert', 'context')), parts along dimension 0, may hold values from -6 to 6
- queries: bfloat16 [32768, 2048], P(('dp', 'expert', 'context')), parts along dimension 0, may hold values from -4.6 to 4.6
- key_vectors: bfloat16 [32768, 256], P(('dp', 'expert', 'context')), parts along dimension 0, may hold values from -5 to 5
- value_vectors: bfloat16 [32768, 256], P(('dp', 'expert', 'context')), parts along dimension 0, may hold values from -5 to 5
- output_weight: bfloat16 [2048, 1024], P('context'), may hold values from -0.875 to 0.875
- norm_gain: float32 [1024], replicated, may hold values from 0.1 to 1.9
- routes: int32 [32768, 8], P(('dp', 'expert', 'context')), parts along dimension 0, may hold values from 0 to 127, all different within a row; in each aligned block of 64 rows (0 to 63, 64 to 127, ...) at most 5 rows name the same one
- gate_levels: int32 [32768, 8], P(('dp', 'expert', 'context')), parts along dimension 0, may hold values from 16 to 96
- expert_in: bfloat16 [256, 1024, 384], P(('context', 'expert')), may hold values from -0.1875 to 0.1875
- expert_out: bfloat16 [256, 192, 1024], P(('context', 'expert')), may hold values from -0.3125 to 0.3125
Outputs:
- layer_out: float32 [32768, 1024], P(('dp', 'expert', 'context')), parts along dimension 0
There are 2 independent parts, one for each index of `dp`. A program takes and returns all parts, laid end to end along the dimension named above; an argument that names none is the same for every part. Nothing has to cross between parts.
Inputs may be any that keep to these rules, and one draw needn't show every extreme that they name: `routes`: in the rows of one device no expert is named more than 5 times, and in every draw some expert reaches 5 in some device's rows; each row names 8 different experts.
All inputs are finite; a program needn't handle non-finite values.
Results may differ from a plain program's by a relative error of at most 0.022.
Values may be sent and summed in bfloat16 or wider, within the bound.
No kernel may reach another device: no remote copies, remote signals or barrier semaphores. Data moves between devices by JAX's collectives and lax.ppermute only.
A program may use at most 192 MiB of HBM per device.

v0:
```python
import math
import jax
import jax.numpy as jnp
import numpy as np
from jax import lax
from jax.sharding import PartitionSpec as P

HD = 128


def expert_apply(gathered, weight_in, weight_out):
    projection = jnp.dot(gathered, weight_in, preferred_element_type=jnp.float32)
    inner_half = weight_in.shape[1] // 2
    activated = (jax.nn.silu(projection[:, :inner_half]) * projection[:, inner_half:]).astype(
        jnp.bfloat16
    )
    return jnp.dot(activated, weight_out, preferred_element_type=jnp.float32).astype(jnp.bfloat16)


def local(
    residual,
    queries,
    key_vectors,
    value_vectors,
    output_weight,
    norm_gain,
    routes,
    gate_levels,
    expert_in,
    expert_out,
):
    context_size = lax.axis_size("context")
    expert_size = lax.axis_size("expert")
    tok_rows, width = residual.shape
    head_count = queries.shape[1] // HD
    key_head_count = key_vectors.shape[1] // HD
    group_size = head_count // key_head_count
    heads_here = head_count // context_size
    keys_here = max(1, heads_here // group_size)
    queries_per_key = min(heads_here, group_size)
    group_rows = tok_rows * context_size
    weight_in = expert_in[0]
    weight_out = expert_out[0]
    head_table = (
        (
            np.arange(context_size)[:, None] * heads_here // group_size
            + np.arange(keys_here)[None, :]
        )
        .reshape(-1)
        .astype(np.int32)
    )
    key_select = key_vectors.reshape(tok_rows, key_head_count, HD)[:, head_table].reshape(
        tok_rows, context_size * keys_here * HD
    )
    value_select = value_vectors.reshape(tok_rows, key_head_count, HD)[:, head_table].reshape(
        tok_rows, context_size * keys_here * HD
    )
    query_local, key_local, value_local = (
        lax.all_to_all(queries, "context", split_axis=1, concat_axis=0, tiled=True),
        lax.all_to_all(key_select, "context", split_axis=1, concat_axis=0, tiled=True),
        lax.all_to_all(value_select, "context", split_axis=1, concat_axis=0, tiled=True),
    )
    own_block = lax.axis_index("expert")
    scaling = 1.0 / math.sqrt(HD)
    to_count = query_local.shape[0]
    query_sets = [
        (
            query_local.reshape(to_count, keys_here, queries_per_key, HD)
            .transpose(1, 0, 2, 3)
            .reshape(keys_here, to_count * queries_per_key, HD),
            own_block * group_rows
            + jnp.arange(group_rows * queries_per_key, dtype=jnp.int32) // queries_per_key,
            (own_block + 1) * group_rows,
        )
    ]
    set_counts = [group_rows]
    initial = tuple(
        (
            (
                jnp.full((keys_here, count * queries_per_key), -1e30, jnp.float32),
                jnp.zeros((keys_here, count * queries_per_key), jnp.float32),
                jnp.zeros((keys_here, count * queries_per_key, HD), jnp.float32),
            )
            for count in set_counts
        )
    )
    start = jnp.int32(0)
    key_piece = lax.all_gather(key_local, "expert", axis=0, tiled=True)
    value_piece = lax.all_gather(value_local, "expert", axis=0, tiled=True)
    piece_rows = key_piece.shape[0]
    key_heads = key_piece.reshape(piece_rows, keys_here, HD).transpose(1, 0, 2)
    value_heads = value_piece.reshape(piece_rows, keys_here, HD).transpose(1, 0, 2)
    key_position = jnp.arange(piece_rows, dtype=jnp.int32)
    updated = []
    for query_set, state in zip(query_sets, initial):
        query_rows, query_position, key_limit = query_set

        def update(inner, query_rows=query_rows, query_position=query_position):
            run_max, run_total, accum = inner
            allowed = (key_position[None, :] <= query_position[:, None])[None]
            scores = (
                jnp.einsum(
                    "grd,gnd->grn", query_rows, key_heads, preferred_element_type=jnp.float32
                )
                * scaling
            )
            masked = jnp.where(allowed, scores, -1e30)
            new_max = jnp.maximum(run_max, jnp.max(masked, axis=2))
            weights = jnp.where(allowed, jnp.exp(masked - new_max[:, :, None]), 0.0)
            run_total = jnp.sum(weights, axis=2)
            accum = jnp.einsum(
                "grn,gnd->grd",
                weights.astype(jnp.bfloat16),
                value_heads,
                preferred_element_type=jnp.float32,
            )
            return (new_max, run_total, accum)

        def unchanged(inner):
            return inner

        updated.append(lax.cond(start < key_limit, update, unchanged, state))
    states = tuple(updated)
    run_max, run_total, accum = states[0]
    result = (accum / run_total[:, :, None]).astype(jnp.bfloat16)
    attention = (
        result.reshape(keys_here, group_rows, queries_per_key, HD)
        .transpose(1, 0, 2, 3)
        .reshape(group_rows, heads_here * HD)
    )
    projected = lax.psum_scatter(
        jnp.dot(attention, output_weight, preferred_element_type=jnp.float32).astype(jnp.bfloat16),
        "context",
        scatter_dimension=0,
        tiled=True,
    ).astype(jnp.float32)
    hidden_state = residual.astype(jnp.float32) + projected
    mean_square = jnp.mean(hidden_state * hidden_state, axis=1, keepdims=True)
    normed = (hidden_state * lax.rsqrt(mean_square + 1e-06) * norm_gain).astype(jnp.bfloat16)
    top_count = routes.shape[1]
    expert_count = expert_size * context_size // 2
    group_experts = expert_size // 2
    capacity = min(tok_rows, max(2, 5 * tok_rows * top_count // (4 * expert_count)))
    slot_count = expert_count * capacity
    flat_routes = routes.reshape(-1)
    expert_hits = (
        flat_routes[:, None] == jnp.arange(expert_count, dtype=jnp.int32)[None, :]
    ).astype(jnp.int32)
    earlier = jnp.cumsum(expert_hits, axis=0) - expert_hits
    target_slot = flat_routes * capacity + jnp.sum(earlier * expert_hits, axis=1)
    placement = (
        target_slot.reshape(tok_rows, top_count)[:, :, None]
        == jnp.arange(slot_count, dtype=jnp.int32)[None, None, :]
    )
    sending = jnp.any(placement, axis=1).astype(jnp.bfloat16)
    outgoing = lax.dot_general(
        sending, normed, (((0,), (0,)), ((), ())), preferred_element_type=jnp.float32
    ).astype(jnp.bfloat16)
    gate_shares = jnp.sum(
        jnp.where(placement, gate_levels[:, :, None].astype(jnp.float32) / 256.0, 0.0), axis=1
    ).astype(jnp.bfloat16)
    arrived = lax.all_to_all(
        outgoing.reshape(context_size, group_experts, capacity, width),
        "context",
        split_axis=0,
        concat_axis=0,
        tiled=True,
    )
    item_count = arrived.shape[2]
    copies = jnp.broadcast_to(
        arrived.transpose(1, 0, 2, 3)[:, None], (group_experts, 2, context_size, item_count, width)
    ).reshape(expert_size, context_size, item_count, width)
    rows_in = lax.all_to_all(copies, "expert", split_axis=0, concat_axis=0, tiled=True)
    partial_out = expert_apply(rows_in.reshape(-1, width), weight_in, weight_out).reshape(
        rows_in.shape
    )
    came_back = lax.all_to_all(partial_out, "expert", split_axis=0, concat_axis=0, tiled=True)
    summed = (
        came_back.reshape(group_experts, 2, context_size, item_count, width)
        .astype(jnp.float32)
        .sum(axis=1)
        .astype(jnp.bfloat16)
    )
    result = summed.transpose(1, 0, 2, 3)
    answers = lax.all_to_all(result, "context", split_axis=0, concat_axis=0, tiled=True)
    moe_sum = jnp.dot(
        gate_shares, answers.reshape(slot_count, width), preferred_element_type=jnp.float32
    )
    return hidden_state + moe_sum


def solution(mesh):
    return jax.shard_map(
        local,
        mesh=mesh,
        in_specs=(
            P(("dp", "expert", "context"), None),
            P(("dp", "expert", "context"), None),
            P(("dp", "expert", "context"), None),
            P(("dp", "expert", "context"), None),
            P("context", None),
            P(),
            P(("dp", "expert", "context"), None),
            P(("dp", "expert", "context"), None),
            P(("context", "expert"), None, None),
            P(("context", "expert"), None, None),
        ),
        out_specs=P(("dp", "expert", "context"), None),
        check_vma=False,
    )
```

profile of v0, /device:TPU:8, one launch (start us, length us, event | category | flops | bytes accessed | tf_op | source)
XLA Modules:
  0.0 555.0 jit_solution(13816407835851833400)
XLA Ops:
  6.5 0.7 pad_clamp_fusion
  7.3 0.8 copy_bitcast_fusion.2
  8.0 0.6 gather_fusion
  8.6 19.3 %all_to_all.68 = bf16[64,8,128]{2,0,1:T(8,128)(2,1)} all-to-all(bf16[64,8,128]{2,0,1:T(8,128)(2,1)S(1)} %bitcast.70), channel_id=1, replica_groups=mesh['context'=8,'expert'=32,'dp'=2] {'context'}, dimensions={1} | all-to-all | bytes 262144 | tf_op jit(solution)/shard_map/all_to_all | solution.py:60
  28.0 0.8 copy_bitcast_fusion.1
  28.8 0.6 gather_fusion.1
  29.3 12.1 %all_to_all.69 = bf16[64,8,128]{2,0,1:T(8,128)(2,1)} all-to-all(bf16[64,8,128]{2,0,1:T(8,128)(2,1)S(1)} %bitcast.69), channel_id=1, replica_groups=mesh['context'=8,'expert'=32,'dp'=2] {'context'}, dimensions={1} | all-to-all | bytes 262144 | tf_op jit(solution)/shard_map/all_to_all | solution.py:61
  41.5 1.7 copy.96
  43.2 3.4 all-to-all-start
  46.6 10.3 %all-to-all-done = bf16[64,8,256]{2,0,1:T(8,128)(2,1)S(1)} async-done(((bf16[64,8,256]{2,0,1:T(8,128)(2,1)}), bf16[64,8,256]{2,0,1:T(8,128)(2,1)S(1)}, u32[]{:S(2)}, u32[]{:S(2)}) %all-to-all-start) | async-done | bytes 262176 | tf_op jit(solution)/shard_map/all_to_all | solution.py:59
  57.0 54.5 %all-gather.3.cloned.1.call-done = bf16[16384,128]{1,0:T(8,128)(2,1)} async-done(((bf16[512,128]{1,0:T(8,128)(2,1)}), bf16[16384,128]{1,0:T(8,128)(2,1)}) %all-gather.3.cloned.1.call-update) | async-done | bytes 4194320 | tf_op jit(solution)/shard_map/all_gather | solution.py:88
  111.5 87.7 %all-gather.5.cloned.1.call-done = bf16[16384,128]{1,0:T(8,128)(2,1)} async-done(((bf16[512,128]{1,0:T(8,128)(2,1)}), bf16[16384,128]{1,0:T(8,128)(2,1)}) %all-gather.5.cloned.1.call-update) | async-done | bytes 4194320 | tf_op jit(solution)/shard_map/all_gather | solution.py:89
  199.3 74.4 %conditional.1 = (f32[1,1024]{1,0:T(1,128)S(1)}, f32[1,1024,128]{2,1,0:T(8,128)S(1)}) conditional(s32[]{:T(128)} %convert_element_type.51, () %tuple.19, (s32[16384]{0:T(1024)S(1)}, s32[]{:T(128)}, s32[1024]{0:T(1024)S(1)}, bf16[8,64,256]{2,1,0:T(8,128)(2,1)S(1)}, bf16[16384,128]{1,0:T(8,128)(2,1)}, /*index=5*/bf16[16384,128]{1,0:T(8,128)(2,1)}) %tuple.32), branch_computations={%region_0.1_spmd, %region_1.4_spmd} | conditional | flops 8858378240 | bytes 211267616 | solution.py:122
  199.3 0.1 reshape.111
  199.4 25.7 %fusion = (f32[1024]{0:T(1024)S(1)}, f32[1024,16384]{1,0:T(8,128)}) fusion(s32[16384]{0:T(1024)S(1)} %get-tuple-element.90, s32[1024]{0:T(1024)S(1)} %fusion.8, bf16[1024,128]{1,0:T(8,128)(2,1)S(1)} %reshape.111, bf16[16384,128]{1,0:T(8,128)(2,1)} %get-tuple-element.94), kind=kOutput, calls=%fused_computation.4 | convolution fusion | flops 4362075136 | bytes 71639040 | tf_op jit(solution)/shard_map/cond/branch_1_fun/grd,gnd->grn/dot_general | solution.py:102
  225.2 26.5 %fusion.5 = f32[1,1024,128]{2,1,0:T(8,128)S(1)} fusion(bf16[16384,128]{1,0:T(8,128)(2,1)} %get-tuple-element.95, f32[1024,16384]{1,0:T(8,128)} %get-tuple-element.113, f32[1024]{0:T(1024)S(1)} %broadcast_maximum_fusion, s32[16384]{0:T(1024)S(1)} %get-tuple-element.90, s32[1024]{0:T(1024)S(1)} %fusion.8), kind=kOutput, calls=%fused_computation.8 | convolution fusion | flops 4395630592 | bytes 71901184 | tf_op jit(solution)/shard_map/cond/branch_1_fun/grn,gnd->grd/dot_general | solution.py:111
  251.6 22.1 %fusion.2 = f32[1024]{0:T(1024)S(1)} fusion(f32[1024,16384]{1,0:T(8,128)} %get-tuple-element.113, f32[1024]{0:T(1024)S(1)} %broadcast_maximum_fusion, s32[16384]{0:T(1024)S(1)} %get-tuple-element.90, s32[1024]{0:T(1024)S(1)} %fusion.8), kind=kLoop, calls=%fused_computation.6 | loop fusion | flops 100662272 | bytes 67186688 | tf_op jit(solution)/shard_map/cond/branch_1_fun/reduce_sum | solution.py:110
  273.8 0.2 divide_convert_fusion
  274.1 1.4 convolution_convert_fusion.2
  275.6 0.1 eq.42
  275.8 0.1 copy.76
  275.9 0.2 fusion.22
  276.2 0.2 fusion.21
  276.7 0.5 fusion.13
  277.2 37.8 %reduce-scatter.2.cloned.1.call-done = bf16[64,1024]{1,0:T(8,128)(2,1)} async-done(((bf16[512,1024]{1,0:T(8,128)(2,1)}), bf16[64,1024]{1,0:T(8,128)(2,1)}) %reduce-scatter.2.cloned.1.call-update) | async-done | bytes 131088 | tf_op jit(solution)/shard_map/reduce_scatter | solution.py:131
  315.0 1.0 multiply_reduce_fusion
  316.1 2.5 convolution_convert_fusion.1
  318.7 2.6 reshape.124
  321.3 0.9 copy.81
  322.2 34.2 %all_to_all.70 = bf16[8,16,5,1024]{3,1,2,0:T(8,128)(2,1)S(1)} all-to-all(bf16[8,16,5,1024]{3,1,2,0:T(8,128)(2,1)S(1)} %copy.81), channel_id=1, replica_groups=mesh['context'=8,'expert'=32,'dp'=2] {'context'}, dimensions={0} | all-to-all | bytes 2621440 | tf_op jit(solution)/shard_map/all_to_all | solution.py:162
  356.4 0.7 copy.82
  357.1 0.3 broadcast_in_dim.54
  357.4 66.3 %all_to_all.71 = bf16[32,8,5,1024]{3,1,2,0:T(8,128)(2,1)S(1)} all-to-all(bf16[32,8,5,1024]{3,1,2,0:T(8,128)(2,1)S(1)} %bitcast.61), channel_id=1, replica_groups=mesh['context'=8,'expert'=32,'dp'=2] {'expert'}, dimensions={0} | all-to-all | bytes 5242880 | tf_op jit(solution)/shard_map/all_to_all | solution.py:173
  423.7 4.0 copy.83
  427.7 4.9 reshape.126
  432.7 1.3 fusion.15
  433.9 0.9 convolution_convert_fusion
  434.8 2.9 reshape.127
  437.7 4.9 copy.84
  442.6 61.2 %all_to_all.72 = bf16[32,8,5,1024]{3,1,2,0:T(8,128)(2,1)S(1)} all-to-all(bf16[32,8,5,1024]{3,1,2,0:T(8,128)(2,1)S(1)} %copy.84), channel_id=1, replica_groups=mesh['context'=8,'expert'=32,'dp'=2] {'expert'}, dimensions={0} | all-to-all | bytes 5242880 | tf_op jit(solution)/shard_map/all_to_all | solution.py:177
  503.8 0.6 bitcast_reduce_fusion
  504.4 1.8 copy.86
  506.2 6.4 %all-to-all-start.6 = ((bf16[8,16,5,1024]{3,1,2,0:T(8,128)(2,1)}), bf16[8,16,5,1024]{3,1,2,0:T(8,128)(2,1)}, u32[]{:S(2)}, u32[]{:S(2)}) async-start(bf16[8,16,5,1024]{3,1,2,0:T(8,128)(2,1)} %copy.86), calls=%async_computation.7 | async-start | bytes 2621440 | tf_op jit(solution)/shard_map/all_to_all | solution.py:185
  512.7 0.5 select_reduce_fusion
  513.2 29.2 %all-to-all-done.6 = bf16[8,16,5,1024]{3,1,2,0:T(8,128)(2,1)} async-done(((bf16[8,16,5,1024]{3,1,2,0:T(8,128)(2,1)}), bf16[8,16,5,1024]{3,1,2,0:T(8,128)(2,1)}, u32[]{:S(2)}, u32[]{:S(2)}) %all-to-all-start.6) | async-done | bytes 1310752 | tf_op jit(solution)/shard_map/all_to_all | solution.py:185
  542.4 2.2 copy.87
  544.6 1.4 reshape.129
  546.1 2.4 convolution_add_fusion
  (46 shorter events, 0.9 us)
Async XLA Ops:
  6.5 426.1 %copy-start = (bf16[1,1024,384]{2,1,0:T(8,128)(2,1)S(1)}, bf16[1,1024,384]{2,1,0:T(8,128)(2,1)}, u32[]{:S(2)}) copy-start(bf16[1,1024,384]{2,1,0:T(8,128)(2,1)} %param.23) | copy-start | bytes 2359300
  6.5 105.0 %all-gather.3.cloned.1.call-start = ((), (), s32[]{:S(2)}) async-start(), calls=%async_computation.8 | async-start | bytes 4325376 | tf_op jit(solution)/shard_map/all_gather | solution.py:88
  28.0 171.3 %all-gather.5.cloned.1.call-start = ((), (), s32[]{:S(2)}) async-start(), calls=%async_computation.9 | async-start | bytes 4325376 | tf_op jit(solution)/shard_map/all_gather | solution.py:89
  43.2 13.8 %all-to-all-start = ((bf16[64,8,256]{2,0,1:T(8,128)(2,1)}), bf16[64,8,256]{2,0,1:T(8,128)(2,1)S(1)}, u32[]{:S(2)}, u32[]{:S(2)}) async-start(bf16[64,8,256]{2,0,1:T(8,128)(2,1)} %bitcast.57), calls=%async_computation | async-start | bytes 524288 | tf_op jit(solution)/shard_map/all_to_all | solution.py:59
  46.6 268.4 %reduce-scatter.2.cloned.1.call-start = ((), (), s32[]{:S(2)}) async-start(), calls=%async_computation.10 | async-start | bytes 1179648 | tf_op jit(solution)/shard_map/reduce_scatter | solution.py:131
  199.3 74.8 %copy-start.3 = (bf16[256,1024]{1,0:T(8,128)(2,1)S(1)}, bf16[256,1024]{1,0:T(8,128)(2,1)}, u32[]{:S(2)}) copy-start(bf16[256,1024]{1,0:T(8,128)(2,1)} %param.19) | copy-start | bytes 1572868
  273.7 1.8 copy-start.6
  273.7 41.3 %copy-start.1 = (bf16[64,1024]{1,0:T(8,128)(2,1)S(1)}, bf16[64,1024]{1,0:T(8,128)(2,1)}, u32[]{:S(2)}) copy-start(bf16[64,1024]{1,0:T(8,128)(2,1)} %param.15) | copy-start | bytes 393220
  273.7 42.4 %copy-start.7 = (f32[1024]{0:T(1024)S(1)}, f32[1024]{0:T(1024)}, u32[]{:S(2)}) copy-start(f32[1024]{0:T(1024)} %param.20) | copy-start | bytes 12292
  276.7 39.4 %copy-start.4 = (s32[64,8]{1,0:T(8,128)}, s32[64,8]{1,0:T(8,128)S(1)}, u32[]{:S(2)}) copy-start(s32[64,8]{1,0:T(8,128)S(1)} %copy.79) | copy-start | bytes 6148
  432.6 1.3 copy-start.9
  503.8 8.8 %copy-start.8 = (s32[64,8]{0,1:T(8,128)S(1)}, s32[64,8]{0,1:T(8,128)}, u32[]{:S(2)}) copy-start(s32[64,8]{0,1:T(8,128)} %param.22) | copy-start | bytes 6148
  503.8 8.9 %copy-start.5 = (s32[64,8]{1,0:T(8,128)S(1)}, s32[64,8]{1,0:T(8,128)}, u32[]{:S(2)}) copy-start(s32[64,8]{1,0:T(8,128)} %copy-done.4) | copy-start | bytes 6148
  506.2 39.9 %copy-start.2 = (bf16[64,1024]{1,0:T(8,128)(2,1)S(1)}, bf16[64,1024]{1,0:T(8,128)(2,1)}, u32[]{:S(2)}) copy-start(bf16[64,1024]{1,0:T(8,128)(2,1)} %reduce-scatter.2.cloned.1.call-done) | copy-start | bytes 393220
  506.2 36.2 %all-to-all-start.6 = ((bf16[8,16,5,1024]{3,1,2,0:T(8,128)(2,1)}), bf16[8,16,5,1024]{3,1,2,0:T(8,128)(2,1)}, u32[]{:S(2)}, u32[]{:S(2)}) async-start(bf16[8,16,5,1024]{3,1,2,0:T(8,128)(2,1)} %copy.86), calls=%async_computation.7 | async-start | bytes 2621440 | tf_op jit(solution)/shard_map/all_to_all | solution.py:185
Sparse Core Ops, SparseCore 0:
  28.1 83.4 all-gather.2
  114.7 84.5 all-gather.4
  275.7 39.3 reduce-scatter.1
where the time goes:
time: 556 us; the launch traced here: 555 us
  waiting for transfers between devices  220 us (40%)
  blocking collectives  193 us (35%)
  matrix products  60.7 us (11%)
  local copies, waits for them, and re-layouts  32 us (6%)
  other arithmetic  26.1 us (5%)
  between operations  13.4 us (2%)
  starting transfers between devices  9.92 us (2%)
    all_gather x1, waiting for transfers between devices, local(): value_piece = lax.all_gather(value_local, 'expert', axis=0, tiled=True)  87.7 us
    all_to_all x1, blocking collectives, local(): lax.all_to_all(copies, 'expert', split_axis=0, concat_axis=0, tiled=True)  66.3 us
    all_to_all x1, blocking collectives, local(): lax.all_to_all(partial_out, 'expert', split_axis=0, concat_axis=0, tiled=...  61.2 us
    all_gather x1, waiting for transfers between devices, local(): key_piece = lax.all_gather(key_local, 'expert', axis=0, tiled=True)  54.5 us
    reduce_scatter x1, waiting for transfers between devices, local(): lax.psum_scatter(jnp.dot(attention, output_weight, preferred_element_type...  37.8 us
    all_to_all x1, blocking collectives, local(): lax.all_to_all(outgoing.reshape(context_size, group_experts, capacity, wi...  34.2 us
    all_to_all x1, waiting for transfers between devices, local(): lax.all_to_all(result, 'context', split_axis=0, concat_axis=0, tiled=True)  29.2 us
    dot_general x1, matrix products, update(): jnp.einsum('grn,gnd->grd', weights.astype(jnp.bfloat16), value_heads, pre...  26.5 us
  transfers between devices with their start and end apart: 5, of which 5 were waited for; matrix products, arithmetic and copies ran while one was open for 1% of the time, Pallas kernels for 0%

commit v1 on v0

--- a/solution.py
+++ b/solution.py
@@ -4,6 +4,7 @@
 import numpy as np
 from jax import lax
 from jax.sharding import PartitionSpec as P
+from jax.lax import all_to_all, axis_size
 
 HD = 128
 
@@ -29,6 +30,13 @@
     expert_in,
     expert_out,
 ):
+
+    def heads_carry(payload):
+        block_now = axis_size("context")
+        placed = jnp.split(payload, block_now, axis=1)
+        q_next = all_to_all(jnp.stack(placed), "context", 0, 0)
+        return jnp.concatenate(q_next, axis=0)
+
     context_size = lax.axis_size("context")
     expert_size = lax.axis_size("expert")
     tok_rows, width = residual.shape
@@ -56,7 +64,7 @@
         tok_rows, context_size * keys_here * HD
     )
     query_local, key_local, value_local = (
-        lax.all_to_all(queries, "context", split_axis=1, concat_axis=0, tiled=True),
+        heads_carry(queries),
         lax.all_to_all(key_select, "context", split_axis=1, concat_axis=0, tiled=True),
         lax.all_to_all(value_select, "context", split_axis=1, concat_axis=0, tiled=True),
     )

time: 556 us -> 556 us (level)
  waiting for transfers between devices: 220 us -> 210 us
  local copies, waits for them, and re-layouts: 32 us -> 41.3 us
    unnamed x22 -> x29, local copies, waits for them, and re-layouts: 0.14 us -> 9.76 us
    all_gather x1, waiting for transfers between devices: 54.5 us -> 45.1 us  [local(): key_piece = lax.all_gather(key_local, 'expert', axis=0, tiled=True)]
  transfers between devices with their start and end apart: 5 -> 5, of which waited for: 5 -> 5; matrix products, arithmetic and copies ran while one was open for 1% -> 3% of each run, Pallas kernels for 0% -> 0%
where the time goes in v1:
time: 556 us; the launch traced here: 554 us
  waiting for transfers between devices  210 us (38%)
  blocking collectives  193 us (35%)
  matrix products  60.7 us (11%)
  local copies, waits for them, and re-layouts  41.3 us (7%)
  other arithmetic  26.1 us (5%)
  between operations  13.4 us (2%)
  starting transfers between devices  9.51 us (2%)
    all_gather x1, waiting for transfers between devices, local(): value_piece = lax.all_gather(value_local, 'expert', axis=0, tiled=True)  87.7 us
    all_to_all x1, blocking collectives, local(): lax.all_to_all(copies, 'expert', split_axis=0, concat_axis=0, tiled=True)  66.3 us
    all_to_all x1, blocking collectives, local(): lax.all_to_all(partial_out, 'expert', split_axis=0, concat_axis=0, tiled=...  61.1 us
    all_gather x1, waiting for transfers between devices, local(): key_piece = lax.all_gather(key_local, 'expert', axis=0, tiled=True)  45.1 us
    reduce_scatter x1, waiting for transfers between devices, local(): lax.psum_scatter(jnp.dot(attention, output_weight, preferred_element_type...  38 us
    all_to_all x1, blocking collectives, local(): lax.all_to_all(outgoing.reshape(context_size, group_experts, capacity, wi...  34.1 us
    all_to_all x1, waiting for transfers between devices, local(): lax.all_to_all(result, 'context', split_axis=0, concat_axis=0, tiled=True)  28.9 us
    dot_general x1, matrix products, update(): jnp.einsum('grn,gnd->grd', weights.astype(jnp.bfloat16), value_heads, pre...  26.5 us
  transfers between devices with their start and end apart: 5, of which 5 were waited for; matrix products, arithmetic and copies ran while one was open for 3% of the time, Pallas kernels for 0%

profile of v1, /device:TPU:8, one launch (start us, length us, event | category | flops | bytes accessed | tf_op | source)
XLA Modules:
  0.0 554.1 jit_solution(5412524585814898275)
XLA Ops:
  6.5 0.7 pad_clamp_fusion
  7.3 0.8 copy_bitcast_fusion.1
  8.0 0.6 gather_fusion
  8.6 19.3 %all_to_all.57 = bf16[64,8,128]{2,0,1:T(8,128)(2,1)} all-to-all(bf16[64,8,128]{2,0,1:T(8,128)(2,1)S(1)} %bitcast.80), channel_id=1, replica_groups=mesh['context'=8,'expert'=32,'dp'=2] {'context'}, dimensions={1} | all-to-all | bytes 262144 | tf_op jit(solution)/shard_map/all_to_all | solution.py:68
  28.0 0.8 copy_bitcast_fusion
  28.8 0.6 gather_fusion.1
  29.3 12.1 %all_to_all.58 = bf16[64,8,128]{2,0,1:T(8,128)(2,1)} all-to-all(bf16[64,8,128]{2,0,1:T(8,128)(2,1)S(1)} %bitcast.79), channel_id=1, replica_groups=mesh['context'=8,'expert'=32,'dp'=2] {'context'}, dimensions={1} | all-to-all | bytes 262144 | tf_op jit(solution)/shard_map/all_to_all | solution.py:69
  41.5 1.4 bitcast_dynamic-update-slice_fusion.7
  42.9 1.4 bitcast_dynamic-update-slice_fusion.6
  44.3 1.4 bitcast_dynamic-update-slice_fusion.5
  45.6 1.4 bitcast_dynamic-update-slice_fusion.4
  47.0 1.4 bitcast_dynamic-update-slice_fusion.3
  48.4 1.4 bitcast_dynamic-update-slice_fusion.2
  49.8 1.4 bitcast_dynamic-update-slice_fusion.1
  51.1 1.4 bitcast_dynamic-update-slice_fusion
  52.5 3.4 all-to-all-start
  56.0 10.3 %all-to-all-done = bf16[8,64,256]{2,1,0:T(8,128)(2,1)S(1)} async-done(((bf16[8,64,256]{2,1,0:T(8,128)(2,1)}), bf16[8,64,256]{2,1,0:T(8,128)(2,1)S(1)}, u32[]{:S(2)}, u32[]{:S(2)}) %all-to-all-start) | async-done | bytes 262176 | tf_op jit(solution)/shard_map/all_to_all | solution.py:37
  66.3 45.1 %all-gather.3.cloned.1.call-done = bf16[16384,128]{1,0:T(8,128)(2,1)} async-done(((bf16[512,128]{1,0:T(8,128)(2,1)}), bf16[16384,128]{1,0:T(8,128)(2,1)}) %all-gather.3.cloned.1.call-update) | async-done | bytes 4194320 | tf_op jit(solution)/shard_map/all_gather | solution.py:96
  111.5 87.7 %all-gather.5.cloned.1.call-done = bf16[16384,128]{1,0:T(8,128)(2,1)} async-done(((bf16[512,128]{1,0:T(8,128)(2,1)}), bf16[16384,128]{1,0:T(8,128)(2,1)}) %all-gather.5.cloned.1.call-update) | async-done | bytes 4194320 | tf_op jit(solution)/shard_map/all_gather | solution.py:97
  199.2 74.4 %conditional.1 = (f32[1,1024]{1,0:T(1,128)S(1)}, f32[1,1024,128]{2,1,0:T(8,128)S(1)}) conditional(s32[]{:T(128)} %convert_element_type.51, () %tuple.19, (s32[16384]{0:T(1024)S(1)}, s32[]{:T(128)}, s32[1024]{0:T(1024)S(1)}, bf16[8,64,256]{2,1,0:T(8,128)(2,1)S(1)}, bf16[16384,128]{1,0:T(8,128)(2,1)}, /*index=5*/bf16[16384,128]{1,0:T(8,128)(2,1)}) %tuple.20), branch_computations={%region_0.1_spmd, %region_1.4_spmd} | conditional | flops 8858378240 | bytes 211267616 | solution.py:130
  199.3 25.7 %fusion = (f32[1024]{0:T(1024)S(1)}, f32[1024,16384]{1,0:T(8,128)}) fusion(s32[16384]{0:T(1024)S(1)} %get-tuple-element.90, s32[1024]{0:T(1024)S(1)} %fusion.8, bf16[1024,128]{1,0:T(8,128)(2,1)S(1)} %reshape.107, bf16[16384,128]{1,0:T(8,128)(2,1)} %get-tuple-element.94), kind=kOutput, calls=%fused_computation.4 | convolution fusion | flops 4362075136 | bytes 71639040 | tf_op jit(solution)/shard_map/cond/branch_1_fun/grd,gnd->grn/dot_general | solution.py:110
  225.0 26.5 %fusion.5 = f32[1,1024,128]{2,1,0:T(8,128)S(1)} fusion(bf16[16384,128]{1,0:T(8,128)(2,1)} %get-tuple-element.95, f32[1024,16384]{1,0:T(8,128)} %get-tuple-element.101, f32[1024]{0:T(1024)S(1)} %broadcast_maximum_fusion, s32[16384]{0:T(1024)S(1)} %get-tuple-element.90, s32[1024]{0:T(1024)S(1)} %fusion.8), kind=kOutput, calls=%fused_computation.8 | convolution fusion | flops 4395630592 | bytes 71901184 | tf_op jit(solution)/shard_map/cond/branch_1_fun/grn,gnd->grd/dot_general | solution.py:119
  251.5 22.1 %fusion.2 = f32[1024]{0:T(1024)S(1)} fusion(f32[1024,16384]{1,0:T(8,128)} %get-tuple-element.101, f32[1024]{0:T(1024)S(1)} %broadcast_maximum_fusion, s32[16384]{0:T(1024)S(1)} %get-tuple-element.90, s32[1024]{0:T(1024)S(1)} %fusion.8), kind=kLoop, calls=%fused_computation.6 | loop fusion | flops 100662272 | bytes 67186688 | tf_op jit(solution)/shard_map/cond/branch_1_fun/reduce_sum | solution.py:118
  273.9 1.4 convolution_convert_fusion.2
  276.6 0.5 fusion.13
  277.1 38.0 %reduce-scatter.2.cloned.1.call-done = bf16[64,1024]{1,0:T(8,128)(2,1)} async-done(((bf16[512,1024]{1,0:T(8,128)(2,1)}), bf16[64,1024]{1,0:T(8,128)(2,1)}) %reduce-scatter.2.cloned.1.call-update) | async-done | bytes 131088 | tf_op jit(solution)/shard_map/reduce_scatter | solution.py:139
  315.0 1.0 multiply_reduce_fusion
  316.1 2.5 convolution_convert_fusion.1
  318.7 2.6 reshape.120
  321.3 0.9 copy.76
  322.2 34.1 %all_to_all.59 = bf16[8,16,5,1024]{3,1,2,0:T(8,128)(2,1)S(1)} all-to-all(bf16[8,16,5,1024]{3,1,2,0:T(8,128)(2,1)S(1)} %copy.76), channel_id=1, replica_groups=mesh['context'=8,'expert'=32,'dp'=2] {'context'}, dimensions={0} | all-to-all | bytes 2621440 | tf_op jit(solution)/shard_map/all_to_all | solution.py:170
  356.3 0.7 copy.77
  357.4 66.3 %all_to_all.60 = bf16[32,8,5,1024]{3,1,2,0:T(8,128)(2,1)S(1)} all-to-all(bf16[32,8,5,1024]{3,1,2,0:T(8,128)(2,1)S(1)} %bitcast.72), channel_id=1, replica_groups=mesh['context'=8,'expert'=32,'dp'=2] {'expert'}, dimensions={0} | all-to-all | bytes 5242880 | tf_op jit(solution)/shard_map/all_to_all | solution.py:181
  423.6 4.0 copy.78
  427.6 4.9 reshape.122
  432.6 1.3 fusion.15
  433.8 0.9 convolution_convert_fusion
  434.8 2.9 reshape.123
  437.6 4.9 copy.79
  442.5 61.1 %all_to_all.61 = bf16[32,8,5,1024]{3,1,2,0:T(8,128)(2,1)S(1)} all-to-all(bf16[32,8,5,1024]{3,1,2,0:T(8,128)(2,1)S(1)} %copy.79), channel_id=1, replica_groups=mesh['context'=8,'expert'=32,'dp'=2] {'expert'}, dimensions={0} | all-to-all | bytes 5242880 | tf_op jit(solution)/shard_map/all_to_all | solution.py:185
  503.6 0.6 bitcast_reduce_fusion
  504.2 1.8 copy.81
  506.1 6.0 %all-to-all-start.6 = ((bf16[8,16,5,1024]{3,1,2,0:T(8,128)(2,1)}), bf16[8,16,5,1024]{3,1,2,0:T(8,128)(2,1)}, u32[]{:S(2)}, u32[]{:S(2)}) async-start(bf16[8,16,5,1024]{3,1,2,0:T(8,128)(2,1)} %copy.81), calls=%async_computation.7 | async-start | bytes 2621440 | tf_op jit(solution)/shard_map/all_to_all | solution.py:193
  512.2 0.5 select_reduce_fusion
  512.7 28.9 %all-to-all-done.6 = bf16[8,16,5,1024]{3,1,2,0:T(8,128)(2,1)} async-done(((bf16[8,16,5,1024]{3,1,2,0:T(8,128)(2,1)}), bf16[8,16,5,1024]{3,1,2,0:T(8,128)(2,1)}, u32[]{:S(2)}, u32[]{:S(2)}) %all-to-all-start.6) | async-done | bytes 1310752 | tf_op jit(solution)/shard_map/all_to_all | solution.py:193
  541.6 2.2 copy.82
  543.8 1.4 reshape.125
  545.2 2.4 convolution_add_fusion
  (53 shorter events, 2.2 us)
Async XLA Ops:
  6.5 426.0 %copy-start = (bf16[1,1024,384]{2,1,0:T(8,128)(2,1)S(1)}, bf16[1,1024,384]{2,1,0:T(8,128)(2,1)}, u32[]{:S(2)}) copy-start(bf16[1,1024,384]{2,1,0:T(8,128)(2,1)} %param.23) | copy-start | bytes 2359300
  6.5 104.9 %all-gather.3.cloned.1.call-start = ((), (), s32[]{:S(2)}) async-start(), calls=%async_computation.8 | async-start | bytes 4325376 | tf_op jit(solution)/shard_map/all_gather | solution.py:96
  28.0 171.2 %all-gather.5.cloned.1.call-start = ((), (), s32[]{:S(2)}) async-start(), calls=%async_computation.9 | async-start | bytes 4325376 | tf_op jit(solution)/shard_map/all_gather | solution.py:97
  52.5 13.8 %all-to-all-start = ((bf16[8,64,256]{2,1,0:T(8,128)(2,1)}), bf16[8,64,256]{2,1,0:T(8,128)(2,1)S(1)}, u32[]{:S(2)}, u32[]{:S(2)}) async-start(bf16[8,64,256]{2,1,0:T(8,128)(2,1)} %bitcast_dynamic-update-slice_fusion), calls=%async_computation | async-start | bytes 524288 | tf_op jit(solution)/shard_map/all_to_all | solution.py:37
  55.9 259.1 %reduce-scatter.2.cloned.1.call-start = ((), (), s32[]{:S(2)}) async-start(), calls=%async_computation.10 | async-start | bytes 1179648 | tf_op jit(solution)/shard_map/reduce_scatter | solution.py:139
  199.2 74.7 %copy-start.3 = (bf16[256,1024]{1,0:T(8,128)(2,1)S(1)}, bf16[256,1024]{1,0:T(8,128)(2,1)}, u32[]{:S(2)}) copy-start(bf16[256,1024]{1,0:T(8,128)(2,1)} %param.19) | copy-start | bytes 1572868
  273.6 1.8 copy-start.6
  273.6 41.4 %copy-start.1 = (bf16[64,1024]{1,0:T(8,128)(2,1)S(1)}, bf16[64,1024]{1,0:T(8,128)(2,1)}, u32[]{:S(2)}) copy-start(bf16[64,1024]{1,0:T(8,128)(2,1)} %param.15) | copy-start | bytes 393220
  273.6 42.5 %copy-start.7 = (f32[1024]{0:T(1024)S(1)}, f32[1024]{0:T(1024)}, u32[]{:S(2)}) copy-start(f32[1024]{0:T(1024)} %param.20) | copy-start | bytes 12292
  276.6 39.5 %copy-start.4 = (s32[64,8]{1,0:T(8,128)}, s32[64,8]{1,0:T(8,128)S(1)}, u32[]{:S(2)}) copy-start(s32[64,8]{1,0:T(8,128)S(1)} %copy.74) | copy-start | bytes 6148
  432.6 1.3 copy-start.9
  503.6 8.4 %copy-start.8 = (s32[64,8]{0,1:T(8,128)S(1)}, s32[64,8]{0,1:T(8,128)}, u32[]{:S(2)}) copy-start(s32[64,8]{0,1:T(8,128)} %param.22) | copy-start | bytes 6148
  503.6 8.5 %copy-start.5 = (s32[64,8]{1,0:T(8,128)S(1)}, s32[64,8]{1,0:T(8,128)}, u32[]{:S(2)}) copy-start(s32[64,8]{1,0:T(8,128)} %copy-done.4) | copy-start | bytes 6148
  506.0 39.2 %copy-start.2 = (bf16[64,1024]{1,0:T(8,128)(2,1)S(1)}, bf16[64,1024]{1,0:T(8,128)(2,1)}, u32[]{:S(2)}) copy-start(bf16[64,1024]{1,0:T(8,128)(2,1)} %reduce-scatter.2.cloned.1.call-done) | copy-start | bytes 393220
  506.1 35.5 %all-to-all-start.6 = ((bf16[8,16,5,1024]{3,1,2,0:T(8,128)(2,1)}), bf16[8,16,5,1024]{3,1,2,0:T(8,128)(2,1)}, u32[]{:S(2)}, u32[]{:S(2)}) async-start(bf16[8,16,5,1024]{3,1,2,0:T(8,128)(2,1)} %copy.81), calls=%async_computation.7 | async-start | bytes 2621440 | tf_op jit(solution)/shard_map/all_to_all | solution.py:193
Sparse Core Ops, SparseCore 0:
  28.1 83.3 all-gather.2
  114.6 84.5 all-gather.4
  275.5 39.4 reduce-scatter.1
